TPU v7x, 256 devices: a whole 4x4x8 slice. The times are simulated.
256 devices in a mesh: ctx: 64 (over z, x, core), rows: 4 (over y).
Axes of the slice: x: 4, y: 4, z: 8, core: 2. Of those that a mesh axis runs over, the one named last changes fastest.
Arguments:
- hidden: bfloat16 [2, 4, 8192], P(None, 'rows'), may hold values from -6 to 6
- norm_gain: bfloat16 [8192], replicated, may hold values from 0.099609375 to 1.8984375
- w_query: bfloat16 [8192, 8192], P(None, 'ctx'), may hold values from -2 to 2
- w_key: bfloat16 [8192, 1024], P(None, 'ctx'), may hold values from -2 to 2
- w_value: bfloat16 [8192, 1024], P(None, 'ctx'), may hold values from -0.0625 to 0.0625
- w_out: bfloat16 [8192, 8192], P('ctx'), may hold values from -0.0625 to 0.0625
- cache_keys: bfloat16 [4, 131072, 8, 128], P('rows', 'ctx'), may hold values from -1200 to 1200
- cache_values: bfloat16 [4, 131072, 8, 128], P('rows', 'ctx'), may hold values from -24 to 24
- lengths: int32 [4], P('rows'), may hold values from 1 to 131072, as said below
- positions: int32 [4], P('rows'), may hold values from 0 to 8191
Outputs:
- attended: bfloat16 [2, 8192, 4], P(None, 'ctx', 'rows')
Inputs may be any that keep to these rules, and one draw needn't show every extreme that they name: `lengths`: one sequence has exactly 131072 live tokens and another at most 32; slots at or past a sequence's length hold entries that must not be read.
All inputs are finite; a program needn't handle non-finite values.
Results may differ from a plain program's by a relative error of at most 0.02.
The roundings to bfloat16 on the way count: a program that leaves them out, or rounds other values in their place, can miss the bound.
Values may be sent and summed in bfloat16 or wider, within the bound.
A program may use at most 64 MiB of HBM per device.

v0:
```python
import math
import jax
import jax.numpy as jnp
from jax import lax
from jax.sharding import PartitionSpec as P

theta_base = 500000.0
epsilon = 1e-05


def in_one_piece(arrays, axis, dim, along):
    widths = [a.shape[along] for a in arrays]
    both = jnp.concatenate(arrays, axis=along)
    whole = lax.all_gather(both, axis, axis=dim, tiled=True)
    return tuple(jnp.split(whole, [sum(widths[:k]) for k in range(1, len(widths))], axis=along))


def in_one_piece_2(arrays, axis, split_dim, concat_dim, along):
    widths = [math.prod(a.shape[along:]) for a in arrays]
    both = jnp.concatenate(
        [a.reshape(*a.shape[:along], w) for a, w in zip(arrays, widths)], axis=along
    )
    whole = lax.all_to_all(both, axis, split_axis=split_dim, concat_axis=concat_dim, tiled=True)
    tiles = jnp.split(whole, [sum(widths[:k]) for k in range(1, len(widths))], axis=along)
    return tuple((b.reshape(*whole.shape[:along], *a.shape[along:]) for a, b in zip(arrays, tiles)))


def in_blocks(shard, dim, peers):
    shape = shard.shape
    tiles = shard.reshape(*shape[:dim], peers, shape[dim] // peers, *shape[dim + 1 :])
    return jnp.moveaxis(tiles, dim, 0)


def sum_at_owner(shard, axis, dim):
    tiles = in_blocks(shard, dim, lax.axis_size(axis))
    arrived = lax.all_to_all(tiles, axis, split_axis=0, concat_axis=0, tiled=True)
    return arrived.sum(axis=0)


def rotate(vectors, places):
    halfway = vectors.shape[-1] // 2
    inverse = theta_base ** (-(jnp.arange(halfway, dtype=jnp.float32) * 2.0 / vectors.shape[-1]))
    angles = places.astype(jnp.float32)[:, None, None] * inverse
    cosines = jnp.cos(angles)
    sines = jnp.sin(angles)
    leading = vectors[..., :halfway]
    trailing = vectors[..., halfway:]
    return jnp.concatenate(
        [leading * cosines - trailing * sines, trailing * cosines + leading * sines], -1
    )


def normalize(inputs, norm_gain):
    scaled = inputs * lax.rsqrt(jnp.mean(inputs * inputs, -1, keepdims=True) + epsilon)
    return (scaled * norm_gain.astype(jnp.float32)).astype(jnp.bfloat16)


def local_part(grouped, cache_keys, cache_values, live_len, block_size, limit, scale_factor):
    row_count, kv_heads, group_size, head_size = grouped.shape

    def one_block(block_index, carried):
        run_max, numer, denom = carried
        key_block = lax.dynamic_slice_in_dim(cache_keys, block_index * block_size, block_size, 1)
        value_block = lax.dynamic_slice_in_dim(
            cache_values, block_index * block_size, block_size, 1
        )
        scores = (
            jnp.einsum("rkgd,rtkd->rkgt", grouped, key_block, preferred_element_type=jnp.float32)
            * scale_factor
        )
        slots = block_index * block_size + jnp.arange(block_size)
        visible = slots[None, None, None, :] < live_len[:, None, None, None]
        scores = jnp.where(visible, scores, -1e30)
        new_max = jnp.maximum(run_max, jnp.max(scores, -1))
        shrink = jnp.exp(run_max - new_max)
        weights = jnp.where(visible, jnp.exp(scores - new_max[..., None]), 0.0)
        denom = denom * shrink + jnp.sum(weights, -1)
        numer = numer * shrink[..., None] + jnp.einsum(
            "rkgt,rtkd->rkgd",
            weights.astype(jnp.bfloat16),
            value_block,
            preferred_element_type=jnp.float32,
        )
        return (new_max, numer, denom)

    initial = (
        jnp.full((row_count, kv_heads, group_size), -1e30, jnp.float32),
        jnp.zeros((row_count, kv_heads, group_size, head_size), jnp.float32),
        jnp.zeros((row_count, kv_heads, group_size), jnp.float32),
    )
    run_max, numer, denom = lax.fori_loop(0, limit, one_block, initial)
    total_heads = kv_heads * group_size
    return (
        run_max.reshape(row_count, total_heads),
        numer.reshape(row_count, total_heads, head_size),
        denom.reshape(row_count, total_heads),
    )


def on_device(
    hidden, norm_gain, w_query, w_key, w_value, w_out, cache_keys, cache_values, lengths, positions
):
    devices = lax.axis_size("ctx")
    ctx_index = lax.axis_index("ctx")
    step_count = hidden.shape[0]
    row_count = hidden.shape[1]
    head_size = cache_keys.shape[3]
    kv_heads = cache_keys.shape[2]
    local_span = cache_keys.shape[1]
    own_heads = w_query.shape[1] // head_size
    total_heads = own_heads * devices
    group_size = total_heads // kv_heads
    scale_factor = 1.0 / math.sqrt(head_size)
    block_size = min(512, local_span)
    limit = local_span // block_size
    live_len = jnp.clip(lengths - ctx_index * local_span, 0, local_span)
    head_start = ctx_index * own_heads
    kv_index = head_start // group_size
    fresh_keys = []
    fresh_values = []
    results = []
    for step_index in range(step_count):
        layer_in = hidden[step_index].astype(jnp.float32)
        normed = normalize(layer_in, norm_gain)
        query_local = jnp.dot(normed, w_query, preferred_element_type=jnp.float32).astype(
            jnp.bfloat16
        )
        key_local = jnp.dot(normed, w_key, preferred_element_type=jnp.float32).astype(jnp.bfloat16)
        value_local = jnp.dot(normed, w_value, preferred_element_type=jnp.float32).astype(
            jnp.bfloat16
        )
        query_all, key_all, value_all = (
            lax.all_gather(query_local, "ctx", axis=1, tiled=True),
            *in_one_piece((key_local, value_local), "ctx", 1, 0),
        )
        places = positions + step_index
        queries = rotate(
            query_all.astype(jnp.float32).reshape(row_count, total_heads, head_size), places
        ).astype(jnp.bfloat16)
        new_keys = rotate(
            key_all.astype(jnp.float32).reshape(row_count, kv_heads, head_size), places
        ).astype(jnp.bfloat16)
        fresh_keys.append(new_keys)
        fresh_values.append(value_all.reshape(row_count, kv_heads, head_size))
        grouped = queries.reshape(row_count, kv_heads, group_size, head_size)
        run_max, numer, denom = local_part(
            grouped, cache_keys, cache_values, live_len, block_size, limit, scale_factor
        )
        got_max, got_num, got_den = tuple(
            (
                part.astype(jnp.float32)
                for part in in_one_piece_2(
                    (
                        run_max.astype(jnp.bfloat16),
                        numer.astype(jnp.bfloat16),
                        denom.astype(jnp.bfloat16),
                    ),
                    "ctx",
                    1,
                    1,
                    2,
                )
            )
        )
        got_max = got_max.reshape(row_count, devices, own_heads)
        got_num = got_num.reshape(row_count, devices, own_heads, head_size)
        got_den = got_den.reshape(row_count, devices, own_heads)
        own_max = jnp.max(got_max, 1)
        factors = jnp.exp(got_max - own_max[:, None, :])
        own_num = jnp.sum(got_num * factors[..., None], 1)
        own_den = jnp.sum(got_den * factors, 1)
        own_query = lax.dynamic_slice_in_dim(queries, head_start, own_heads, 1)
        stacked_keys = lax.dynamic_index_in_dim(
            jnp.stack(fresh_keys, 1), kv_index, 2, keepdims=False
        )
        stacked_values = lax.dynamic_index_in_dim(
            jnp.stack(fresh_values, 1), kv_index, 2, keepdims=False
        )
        fresh_scores = (
            jnp.einsum("rjd,rtd->rjt", own_query, stacked_keys, preferred_element_type=jnp.float32)
            * scale_factor
        )
        final_max = jnp.maximum(own_max, jnp.max(fresh_scores, -1))
        shrink = jnp.exp(own_max - final_max)
        fresh_weights = jnp.exp(fresh_scores - final_max[..., None])
        final_den = own_den * shrink + jnp.sum(fresh_weights, -1)
        final_num = own_num * shrink[..., None] + jnp.einsum(
            "rjt,rtd->rjd",
            fresh_weights.astype(jnp.bfloat16),
            stacked_values,
            preferred_element_type=jnp.float32,
        )
        head_out = (
            (final_num / final_den[..., None])
            .astype(jnp.bfloat16)
            .reshape(row_count, own_heads * head_size)
        )
        summed = sum_at_owner(
            lax.dot_general(
                w_out, head_out, (((0,), (1,)), ((), ())), preferred_element_type=jnp.float32
            ),
            "ctx",
            0,
        )
        results.append(summed.astype(jnp.bfloat16))
    return jnp.stack(results, 0)


def solution(mesh):
    in_specs = (
        P(None, "rows", None),
        P(),
        P(None, "ctx"),
        P(None, "ctx"),
        P(None, "ctx"),
        P("ctx", None),
        P("rows", "ctx", None, None),
        P("rows", "ctx", None, None),
        P("rows"),
        P("rows"),
    )
    out_specs = P(None, "ctx", "rows")
    return jax.shard_map(
        on_device, mesh=mesh, in_specs=in_specs, out_specs=out_specs, check_vma=False
    )
```

profile of v0, /device:TPU:1, one launch (start us, length us, event | category | flops | bytes accessed | tf_op | source)
XLA Modules:
  0.0 265.3 jit_solution(8186538398806153378)
XLA Ops:
  0.0 1.7 multiply_reduce_fusion.1
  3.1 0.9 convert_multiply_fusion.3
  4.0 0.7 fusion.65
  5.5 2.0 fusion.59
  7.5 44.0 %all-gather.2 = bf16[64,1,128]{2,1,0:T(2,128)(2,1)S(1)} all-gather(bf16[1,1,128]{2,1,0:T(2,128)(2,1)S(1)} %fusion.59), channel_id=2, replica_groups=mesh['ctx'=64,'rows'=4] {'ctx'}, dimensions={0}, use_global_device_ids=true | all-gather | bytes 16640 | tf_op jit(solution)/shard_map/all_gather | solution.py:133
  52.1 4.8 %copy.55 = bf16[1,2048,8,128]{3,1,2,0:T(8,128)(2,1)} copy(bf16[1,2048,8,128]{3,2,1,0:T(8,128)(2,1)} %param.20) | data formatting | bytes 8388608
  57.0 2.6 copy.56
  59.8 14.0 %while.36 = (s32[]{:T(128)}, f32[1,8,8]{2,1,0:T(8,128)S(1)}, f32[1,8,8,128]{3,2,1,0:T(8,128)S(1)}, f32[1,8,8]{2,1,0:T(8,128)S(1)}, s32[1]{0:T(128)}, /*index=5*/...) while((s32[]{:T(128)}, f32[1,8,8]{2,1,0:T(8,128)S(1)}, ...), condition=%wide.region_4.5_spmd.clone, body=%wide.region_1.4_spmd.clone.sunk | while | flops 17098120 | bytes 2578623 | solution.py:91
  59.8 1.7 fusion.143
  61.6 1.6 fusion.145
  63.1 0.2 fusion.146
  63.3 1.7 fusion.143
  65.0 1.6 fusion.145
  66.6 0.2 fusion.146
  66.8 1.7 fusion.143
  68.5 1.6 fusion.145
  70.1 0.2 fusion.146
  70.3 1.7 fusion.143
  72.0 1.6 fusion.145
  73.6 0.2 fusion.146
  74.1 0.7 copy.59
  74.8 6.4 %all-to-all-start = ((bf16[1,64,130]{2,0,1:T(2,128)(2,1)}), bf16[1,64,130]{2,0,1:T(2,128)(2,1)S(1)}, u32[]{:S(2)}, u32[]{:S(2)}) async-start(bf16[1,64,130]{2,0,1:T(2,128)(2,1)} %copy.59), calls=%async_computation | async-start | bytes 131072 | tf_op jit(solution)/shard_map/all_to_all | solution.py:23
  81.2 0.2 fusion.55
  81.4 0.2 fusion.57
  81.7 0.2 fusion.49
  81.9 0.2 fusion.51
  82.1 2.0 fusion.53
  84.1 41.3 %all-gather.3 = bf16[64,16,2]{1,2,0:T(2,128)(2,1)S(1)} all-gather(bf16[1,16,2]{1,2,0:T(2,128)(2,1)S(1)} %maximum_bitcast_fusion), channel_id=1, replica_groups=mesh['ctx'=64,'rows'=4] {'ctx'}, dimensions={0}, use_global_device_ids=true | all-gather | bytes 4160 | tf_op jit(solution)/shard_map/all_gather | solution.py:14
  125.4 0.1 reshape.834
  125.5 37.3 %all-gather.5 = bf16[64,16,2]{1,2,0:T(2,128)(2,1)S(1)} all-gather(bf16[1,16,2]{1,2,0:T(2,128)(2,1)S(1)} %maximum_bitcast_fusion.1), channel_id=1, replica_groups=mesh['ctx'=64,'rows'=4] {'ctx'}, dimensions={0}, use_global_device_ids=true | all-gather | bytes 4160 | tf_op jit(solution)/shard_map/all_gather | solution.py:14
  162.9 0.1 reshape.838
  163.2 38.0 %all-gather.4 = bf16[64,1,128]{2,1,0:T(2,128)(2,1)S(1)} all-gather(bf16[1,1,128]{2,1,0:T(2,128)(2,1)S(1)} %fusion.53), channel_id=3, replica_groups=mesh['ctx'=64,'rows'=4] {'ctx'}, dimensions={0}, use_global_device_ids=true | all-gather | bytes 16640 | tf_op jit(solution)/shard_map/all_gather | solution.py:133
  201.5 13.9 %while.37 = (s32[]{:T(128)}, f32[1,8,8]{2,1,0:T(8,128)S(1)}, f32[1,8,8,128]{3,2,1,0:T(8,128)S(1)}, f32[1,8,8]{2,1,0:T(8,128)S(1)}, s32[1]{0:T(128)}, /*index=5*/...) while((s32[]{:T(128)}, f32[1,8,8]{2,1,0:T(8,128)S(1)}, ...), condition=%wide.region_13.14_spmd.clone, body=%wide.region_10.13_spmd.clone.sunk | while | flops 17098120 | bytes 2578623 | solution.py:91
  201.5 1.7 fusion.149
  203.2 1.6 fusion.151
  204.7 0.2 fusion.152
  205.0 1.7 fusion.149
  206.7 1.6 fusion.151
  208.2 0.2 fusion.152
  208.5 1.7 fusion.149
  210.2 1.6 fusion.151
  211.7 0.2 fusion.152
  212.0 1.7 fusion.149
  213.7 1.6 fusion.151
  215.2 0.2 fusion.152
  215.7 0.8 fusion.114
  216.7 0.7 copy.65
  217.3 0.7 fusion.83
  218.7 5.7 %all-to-all-start.2 = ((bf16[1,64,130]{2,0,1:T(2,128)(2,1)}), bf16[1,64,130]{2,0,1:T(2,128)(2,1)S(1)}, u32[]{:S(2)}, u32[]{:S(2)}) async-start(bf16[1,64,130]{2,0,1:T(2,128)(2,1)} %copy.65), calls=%async_computation.2 | async-start | bytes 131072 | tf_op jit(solution)/shard_map/all_to_all | solution.py:23
  224.3 0.7 slice_reduce_fusion.1
  225.7 1.0 fusion.72
  227.4 0.2 fusion.71
  227.7 1.0 fusion.42
  228.7 5.8 %all-to-all-done.2 = bf16[1,64,130]{2,0,1:T(2,128)(2,1)S(1)} async-done(((bf16[1,64,130]{2,0,1:T(2,128)(2,1)}), bf16[1,64,130]{2,0,1:T(2,128)(2,1)S(1)}, u32[]{:S(2)}, u32[]{:S(2)}) %all-to-all-start.2) | async-done | bytes 16672 | tf_op jit(solution)/shard_map/all_to_all | solution.py:23
  234.4 4.5 %all-to-all-start.1 = ((f32[64,128,1]{1,2,0:T(1,128)}), f32[64,128,1]{1,2,0:T(1,128)S(1)}, u32[]{:S(2)}, u32[]{:S(2)}) async-start(f32[64,128,1]{1,2,0:T(1,128)} %fusion.42), calls=%async_computation.1 | async-start | bytes 65536 | tf_op jit(solution)/shard_map/all_to_all | solution.py:36
  239.0 0.7 slice_reduce_fusion
  240.9 0.6 fusion.109
  241.5 1.0 fusion.74
  243.7 0.2 fusion.73
  243.9 1.1 fusion.45
  245.0 3.3 %all-to-all-done.1 = f32[64,128,1]{1,2,0:T(1,128)S(1)} async-done(((f32[64,128,1]{1,2,0:T(1,128)}), f32[64,128,1]{1,2,0:T(1,128)S(1)}, u32[]{:S(2)}, u32[]{:S(2)}) %all-to-all-start.1) | async-done | bytes 32800 | tf_op jit(solution)/shard_map/all_to_all | solution.py:36
  248.3 7.0 %all-to-all-start.3 = ((f32[64,128,1]{1,2,0:T(1,128)}), f32[64,128,1]{1,2,0:T(1,128)S(1)}, u32[]{:S(2)}, u32[]{:S(2)}) async-start(f32[64,128,1]{1,2,0:T(1,128)} %fusion.45), calls=%async_computation.3 | async-start | bytes 65536 | tf_op jit(solution)/shard_map/all_to_all | solution.py:36
  255.4 9.3 %all-to-all-done.3 = f32[64,128,1]{1,2,0:T(1,128)S(1)} async-done(((f32[64,128,1]{1,2,0:T(1,128)}), f32[64,128,1]{1,2,0:T(1,128)S(1)}, u32[]{:S(2)}, u32[]{:S(2)}) %all-to-all-start.3) | async-done | bytes 32800 | tf_op jit(solution)/shard_map/all_to_all | solution.py:36
  264.8 0.5 copy.69
  (81 shorter events, 1.9 us)
Async XLA Ops:
  0.0 227.7 %copy-start = (bf16[128,8192]{1,0:T(8,128)(2,1)S(1)}, bf16[128,8192]{1,0:T(8,128)(2,1)}, u32[]{:S(2)}) copy-start(bf16[128,8192]{1,0:T(8,128)(2,1)} %param.19) | copy-start | bytes 6291460
  52.1 4.8 %copy-start.1 = (bf16[1,2048,8,128]{3,2,1,0:T(8,128)(2,1)S(1)}, bf16[1,2048,8,128]{3,2,1,0:T(8,128)(2,1)}, u32[]{:S(2)}) copy-start(bf16[1,2048,8,128]{3,2,1,0:T(8,128)(2,1)} %param.21) | copy-start | bytes 12582916
  59.8 21.5 %copy-start.2 = (bf16[8192,16]{0,1:T(8,128)(2,1)S(1)}, bf16[8192,16]{0,1:T(8,128)(2,1)}, u32[]{:S(2)}) copy-start(bf16[8192,16]{0,1:T(8,128)(2,1)} %param.18) | copy-start | bytes 786436
  59.8 21.7 %copy-start.3 = (bf16[8192,16]{0,1:T(8,128)(2,1)S(1)}, bf16[8192,16]{0,1:T(8,128)(2,1)}, u32[]{:S(2)}) copy-start(bf16[8192,16]{0,1:T(8,128)(2,1)} %param.17) | copy-start | bytes 786436
  74.8 143.9 %all-to-all-start = ((bf16[1,64,130]{2,0,1:T(2,128)(2,1)}), bf16[1,64,130]{2,0,1:T(2,128)(2,1)S(1)}, u32[]{:S(2)}, u32[]{:S(2)}) async-start(bf16[1,64,130]{2,0,1:T(2,128)(2,1)} %copy.59), calls=%async_computation | async-start | bytes 131072 | tf_op jit(solution)/shard_map/all_to_all | solution.py:23
  218.7 15.7 %all-to-all-start.2 = ((bf16[1,64,130]{2,0,1:T(2,128)(2,1)}), bf16[1,64,130]{2,0,1:T(2,128)(2,1)S(1)}, u32[]{:S(2)}, u32[]{:S(2)}) async-start(bf16[1,64,130]{2,0,1:T(2,128)(2,1)} %copy.65), calls=%async_computation.2 | async-start | bytes 131072 | tf_op jit(solution)/shard_map/all_to_all | solution.py:23
  234.4 13.9 %all-to-all-start.1 = ((f32[64,128,1]{1,2,0:T(1,128)}), f32[64,128,1]{1,2,0:T(1,128)S(1)}, u32[]{:S(2)}, u32[]{:S(2)}) async-start(f32[64,128,1]{1,2,0:T(1,128)} %fusion.42), calls=%async_computation.1 | async-start | bytes 65536 | tf_op jit(solution)/shard_map/all_to_all | solution.py:36
  248.3 16.4 %all-to-all-start.3 = ((f32[64,128,1]{1,2,0:T(1,128)}), f32[64,128,1]{1,2,0:T(1,128)S(1)}, u32[]{:S(2)}, u32[]{:S(2)}) async-start(f32[64,128,1]{1,2,0:T(1,128)} %fusion.45), calls=%async_computation.3 | async-start | bytes 65536 | tf_op jit(solution)/shard_map/all_to_all | solution.py:36
where the time goes:
time: 267 us; the launch traced here: 265 us
  blocking collectives  161 us (60%)
  matrix products  33.6 us (13%)
  starting transfers between devices  23.6 us (9%)
  waiting for transfers between devices  18.3 us (7%)
  other arithmetic  11.3 us (4%)
  local copies, waits for them, and re-layouts  9.95 us (4%)
  between operations  7.52 us (3%)
    all_gather x2, blocking collectives, on_device(): lax.all_gather(query_local, 'ctx', axis=1, tiled=True)  82 us
    all_gather x2, blocking collectives, in_one_piece(): whole = lax.all_gather(both, axis, axis=dim, tiled=True)  78.6 us
    dot_general x8, matrix products, one_block(): jnp.einsum('rkgd,rtkd->rkgt', grouped, key_block, preferred_element_type=...  13.5 us
    all_to_all x2, waiting for transfers between devices, sum_at_owner(): lax.all_to_all(tiles, axis, split_axis=0, concat_axis=0, tiled=True)  12.6 us
    dot_general x8, matrix products, one_block(): jnp.einsum('rkgt,rtkd->rkgd', weights.astype(jnp.bfloat16), value_block,...  12.4 us
    all_to_all x2, starting transfers between devices, in_one_piece_2(): lax.all_to_all(both, axis, split_axis=split_dim, concat_axis=concat_dim,...  12.1 us
    all_to_all x2, starting transfers between devices, sum_at_owner(): lax.all_to_all(tiles, axis, split_axis=0, concat_axis=0, tiled=True)  11.5 us
    unnamed x12, local copies, waits for them, and re-layouts  7.67 us
  transfers between devices with their start and end apart: 4, of which 3 were waited for; matrix products, arithmetic and copies ran while one was open for 10% of the time, Pallas kernels for 0%

commit v1 on v0

--- a/solution.py
+++ b/solution.py
@@ -6,6 +6,18 @@
 
 theta_base = 500000.0
 epsilon = 1e-05
+
+
+def collect(x, axis, dim):
+    ways, here = (lax.axis_size(axis), lax.axis_index(axis))
+    grown, reach = (x, 1)
+    while reach < ways:
+        theirs = lax.ppermute(grown, axis, [(d, d ^ reach) for d in range(ways)])
+        mine_first = jnp.concatenate([grown, theirs], axis=dim)
+        theirs_first = jnp.concatenate([theirs, grown], axis=dim)
+        grown = jnp.where(here & reach == 0, mine_first, theirs_first)
+        reach = 2 * reach
+    return grown
 
 
 def in_one_piece(arrays, axis, dim, along):
@@ -130,7 +142,7 @@
             jnp.bfloat16
         )
         query_all, key_all, value_all = (
-            lax.all_gather(query_local, "ctx", axis=1, tiled=True),
+            collect(query_local, "ctx", 1),
             *in_one_piece((key_local, value_local), "ctx", 1, 0),
         )
         places = positions + step_index

time: 267 us -> 216 us (0.81)
  blocking collectives: 161 us -> 78.6 us
  starting transfers between devices: 23.6 us -> 51.1 us
  waiting for transfers between devices: 18.3 us -> 23.2 us
    all_gather x2 -> x0, blocking collectives: 82 us -> none  [on_device(): lax.all_gather(query_local, 'ctx', axis=1, tiled=True)]
    ppermute x0 -> x12, starting transfers between devices: none -> 17.4 us  [collect(): theirs = lax.ppermute(grown, axis, [(d, d ^ reach) for d in range(ways)])]
    all_to_all x2, starting transfers between devices: 12.1 us -> 22.2 us  [in_one_piece_2(): lax.all_to_all(both, axis, split_axis=split_dim, concat_axis=concat_dim,...]
    ppermute x0 -> x12, waiting for transfers between devices: none -> 4.88 us  [collect(): theirs = lax.ppermute(grown, axis, [(d, d ^ reach) for d in range(ways)])]
    unnamed x12 -> x14, local copies, waits for them, and re-layouts: 7.67 us -> 7.68 us
  transfers between devices with their start and end apart: 4 -> 16, of which waited for: 3 -> 9; matrix products, arithmetic and copies ran while one was open for 10% -> 22% of each run, Pallas kernels for 0% -> 0%
where the time goes in v1:
time: 216 us; the launch traced here: 215 us
  blocking collectives  78.6 us (36%)
  starting transfers between devices  51.1 us (24%)
  matrix products  32 us (15%)
  waiting for transfers between devices  23.2 us (11%)
  other arithmetic  11.9 us (6%)
  local copies, waits for them, and re-layouts  10 us (5%)
  between operations  7.73 us (4%)
    all_gather x2, blocking collectives, in_one_piece(): whole = lax.all_gather(both, axis, axis=dim, tiled=True)  78.6 us
    all_to_all x2, starting transfers between devices, in_one_piece_2(): lax.all_to_all(both, axis, split_axis=split_dim, concat_axis=concat_dim,...  22.2 us
    ppermute x12, starting transfers between devices, collect(): theirs = lax.ppermute(grown, axis, [(d, d ^ reach) for d in range(ways)])  17.4 us
    dot_general x8, matrix products, one_block(): jnp.einsum('rkgd,rtkd->rkgt', grouped, key_block, preferred_element_type=...  13.5 us
    all_to_all x2, waiting for transfers between devices, sum_at_owner(): lax.all_to_all(tiles, axis, split_axis=0, concat_axis=0, tiled=True)  12.6 us
    dot_general x8, matrix products, one_block(): jnp.einsum('rkgt,rtkd->rkgd', weights.astype(jnp.bfloat16), value_block,...  12.4 us
    all_to_all x2, starting transfers between devices, sum_at_owner(): lax.all_to_all(tiles, axis, split_axis=0, concat_axis=0, tiled=True)  11.5 us
    unnamed x14, local copies, waits for them, and re-layouts  7.68 us
  transfers between devices with their start and end apart: 16, of which 9 were waited for; matrix products, arithmetic and copies ran while one was open for 22% of the time, Pallas kernels for 0%

profile of v1, /device:TPU:1, one launch (start us, length us, event | category | flops | bytes accessed | tf_op | source)
XLA Modules:
  0.0 214.9 jit_solution(5077157894162417466)
XLA Ops:
  0.0 1.7 multiply_reduce_fusion.1
  3.1 1.0 convert_multiply_fusion.3
  4.1 0.7 fusion.63
  4.9 2.0 fusion.57
  6.9 3.3 %collective-permute-start = (bf16[1,128]{1,0:T(2,128)(2,1)S(1)}, bf16[1,128]{1,0:T(2,128)(2,1)S(1)}, u32[]{:S(2)}, u32[]{:S(2)}) collective-permute-start(bf16[1,128]{1,0:T(2,128)(2,1)S(1)} %bitcast.334), channel_id=1, source_target_pairs={{0,4},{4,0},{8,12},{12,8},{16,20},{20,16},{24,28},{28,24},{32,36},... | collective-permute-start | bytes 776 | tf_op jit(solution)/shard_map/ppermute | solution.py:15
  10.3 0.4 fusion.52
  11.2 0.2 fusion.56
  12.4 41.2 %all-gather = bf16[64,16,2]{1,2,0:T(2,128)(2,1)S(1)} all-gather(bf16[1,16,2]{1,2,0:T(2,128)(2,1)S(1)} %maximum_bitcast_fusion), channel_id=1, replica_groups=mesh['ctx'=64,'rows'=4] {'ctx'}, dimensions={0}, use_global_device_ids=true | all-gather | bytes 4160 | tf_op jit(solution)/shard_map/all_gather | solution.py:26
  53.7 37.3 %all-gather.1 = bf16[64,16,2]{1,2,0:T(2,128)(2,1)S(1)} all-gather(bf16[1,16,2]{1,2,0:T(2,128)(2,1)S(1)} %maximum_bitcast_fusion.1), channel_id=1, replica_groups=mesh['ctx'=64,'rows'=4] {'ctx'}, dimensions={0}, use_global_device_ids=true | all-gather | bytes 4160 | tf_op jit(solution)/shard_map/all_gather | solution.py:26
  91.8 4.8 %copy.55 = bf16[1,2048,8,128]{3,1,2,0:T(8,128)(2,1)} copy(bf16[1,2048,8,128]{3,2,1,0:T(8,128)(2,1)} %param.20) | data formatting | bytes 8388608
  96.6 2.6 %copy.56 = bf16[1,2048,8,128]{3,1,2,0:T(8,128)(2,1)} copy(bf16[1,2048,8,128]{3,2,1,0:T(8,128)(2,1)S(1)} %copy-done.2) | data formatting | bytes 8388608
  99.7 1.0 collective-permute-start.1
  100.7 0.6 collective-permute-start.7
  101.4 0.8 collective-permute-done.1
  102.2 1.8 collective-permute-start.2
  104.0 1.4 collective-permute-start.8
  105.5 0.8 collective-permute-done.2
  106.5 1.8 collective-permute-done.8
  108.4 0.3 collective-permute-start.9
  108.9 1.6 collective-permute-start.4
  110.5 0.4 collective-permute-done.9
  110.9 1.6 collective-permute-start.10
  112.7 3.1 %collective-permute-start.5 = (bf16[1,4096]{1,0:T(2,128)(2,1)S(1)}, bf16[1,4096]{1,0:T(2,128)(2,1)S(1)}, u32[]{:S(2)}, u32[]{:S(2)}) collective-permute-start(bf16[1,4096]{1,0:T(2,128)(2,1)S(1)} %broadcast_select_fusion.1), channel_id=1, source_target_pairs={{0,128},{4,132},{8,136},{12,140},{16,144},{20,148},{24,152},{28,15... | collective-permute-start | bytes 24584 | tf_op jit(solution)/shard_map/ppermute | solution.py:15
  115.8 2.4 %collective-permute-start.11 = (bf16[1,4096]{1,0:T(2,128)(2,1)S(1)}, bf16[1,4096]{1,0:T(2,128)(2,1)S(1)}, u32[]{:S(2)}, u32[]{:S(2)}) collective-permute-start(bf16[1,4096]{1,0:T(2,128)(2,1)S(1)} %broadcast_select_fusion), channel_id=1, source_target_pairs={{0,128},{4,132},{8,136},{12,140},{16,144},{20,148},{24,152},{28,15... | collective-permute-start | bytes 24584 | tf_op jit(solution)/shard_map/ppermute | solution.py:15
  118.3 0.9 collective-permute-done.5
  119.5 13.9 %while.36 = (s32[]{:T(128)}, f32[1,8,8]{2,1,0:T(8,128)S(1)}, f32[1,8,8,128]{3,2,1,0:T(8,128)S(1)}, f32[1,8,8]{2,1,0:T(8,128)S(1)}, s32[1]{0:T(128)}, /*index=5*/...) while((s32[]{:T(128)}, f32[1,8,8]{2,1,0:T(8,128)S(1)}, ...), condition=%wide.region_4.5_spmd.clone, body=%wide.region_1.4_spmd.clone.sunk | while | flops 17098120 | bytes 2578623 | solution.py:103
  119.5 1.7 fusion.145
  121.2 1.6 fusion.147
  123.0 1.7 fusion.145
  124.7 1.6 fusion.147
  126.5 1.7 fusion.145
  128.2 1.6 fusion.147
  130.0 1.7 fusion.145
  131.7 1.6 fusion.147
  133.7 0.7 copy.59
  134.4 11.9 %all-to-all-start = ((bf16[1,64,130]{2,0,1:T(2,128)(2,1)}), bf16[1,64,130]{2,0,1:T(2,128)(2,1)S(1)}, u32[]{:S(2)}, u32[]{:S(2)}) async-start(bf16[1,64,130]{2,0,1:T(2,128)(2,1)} %copy.59), calls=%async_computation | async-start | bytes 131072 | tf_op jit(solution)/shard_map/all_to_all | solution.py:35
  146.5 13.9 %while.37 = (s32[]{:T(128)}, f32[1,8,8]{2,1,0:T(8,128)S(1)}, f32[1,8,8,128]{3,2,1,0:T(8,128)S(1)}, f32[1,8,8]{2,1,0:T(8,128)S(1)}, s32[1]{0:T(128)}, /*index=5*/...) while((s32[]{:T(128)}, f32[1,8,8]{2,1,0:T(8,128)S(1)}, ...), condition=%wide.region_13.14_spmd.clone, body=%wide.region_10.13_spmd.clone.sunk | while | flops 17098120 | bytes 2578623 | solution.py:103
  146.5 1.7 fusion.151
  148.2 1.6 fusion.153
  150.0 1.7 fusion.151
  151.7 1.6 fusion.153
  153.5 1.7 fusion.151
  155.2 1.6 fusion.153
  157.0 1.7 fusion.151
  158.7 1.6 fusion.153
  160.7 0.8 fusion.116
  161.6 0.7 copy.65
  162.2 0.7 fusion.85
  163.6 10.3 %all-to-all-start.2 = ((bf16[1,64,130]{2,0,1:T(2,128)(2,1)}), bf16[1,64,130]{2,0,1:T(2,128)(2,1)S(1)}, u32[]{:S(2)}, u32[]{:S(2)}) async-start(bf16[1,64,130]{2,0,1:T(2,128)(2,1)} %copy.65), calls=%async_computation.2 | async-start | bytes 131072 | tf_op jit(solution)/shard_map/all_to_all | solution.py:35
  173.9 0.7 slice_reduce_fusion.1
  175.3 1.0 fusion.70
  177.0 0.2 fusion.69
  177.2 1.0 fusion.42
  178.2 5.8 %all-to-all-done.2 = bf16[1,64,130]{2,0,1:T(2,128)(2,1)S(1)} async-done(((bf16[1,64,130]{2,0,1:T(2,128)(2,1)}), bf16[1,64,130]{2,0,1:T(2,128)(2,1)S(1)}, u32[]{:S(2)}, u32[]{:S(2)}) %all-to-all-start.2) | async-done | bytes 16672 | tf_op jit(solution)/shard_map/all_to_all | solution.py:35
  184.0 4.5 %all-to-all-start.1 = ((f32[64,128,1]{1,2,0:T(1,128)}), f32[64,128,1]{1,2,0:T(1,128)S(1)}, u32[]{:S(2)}, u32[]{:S(2)}) async-start(f32[64,128,1]{1,2,0:T(1,128)} %fusion.42), calls=%async_computation.1 | async-start | bytes 65536 | tf_op jit(solution)/shard_map/all_to_all | solution.py:48
  188.5 0.7 slice_reduce_fusion
  190.4 0.6 fusion.111
  191.0 1.0 fusion.72
  193.3 0.2 fusion.71
  193.5 1.1 fusion.45
  194.6 3.3 %all-to-all-done.1 = f32[64,128,1]{1,2,0:T(1,128)S(1)} async-done(((f32[64,128,1]{1,2,0:T(1,128)}), f32[64,128,1]{1,2,0:T(1,128)S(1)}, u32[]{:S(2)}, u32[]{:S(2)}) %all-to-all-start.1) | async-done | bytes 32800 | tf_op jit(solution)/shard_map/all_to_all | solution.py:48
  197.9 7.0 %all-to-all-start.3 = ((f32[64,128,1]{1,2,0:T(1,128)}), f32[64,128,1]{1,2,0:T(1,128)S(1)}, u32[]{:S(2)}, u32[]{:S(2)}) async-start(f32[64,128,1]{1,2,0:T(1,128)} %fusion.45), calls=%async_computation.3 | async-start | bytes 65536 | tf_op jit(solution)/shard_map/all_to_all | solution.py:48
  205.0 9.3 %all-to-all-done.3 = f32[64,128,1]{1,2,0:T(1,128)S(1)} async-done(((f32[64,128,1]{1,2,0:T(1,128)}), f32[64,128,1]{1,2,0:T(1,128)S(1)}, u32[]{:S(2)}, u32[]{:S(2)}) %all-to-all-start.3) | async-done | bytes 32800 | tf_op jit(solution)/shard_map/all_to_all | solution.py:48
  214.4 0.5 copy.69
  (147 shorter events, 5.1 us)
Async XLA Ops:
  0.0 177.2 %copy-start = (bf16[128,8192]{1,0:T(8,128)(2,1)S(1)}, bf16[128,8192]{1,0:T(8,128)(2,1)}, u32[]{:S(2)}) copy-start(bf16[128,8192]{1,0:T(8,128)(2,1)} %param.19) | copy-start | bytes 6291460
  3.1 7.1 %copy-start.1 = (bf16[8192,128]{1,0:T(8,128)(2,1)S(1)}, bf16[8192,128]{1,0:T(8,128)(2,1)}, u32[]{:S(2)}) copy-start(bf16[8192,128]{1,0:T(8,128)(2,1)} %param.16) | copy-start | bytes 6291460
  4.9 5.9 %copy-start.3 = (bf16[8192,16]{0,1:T(8,128)(2,1)S(1)}, bf16[8192,16]{0,1:T(8,128)(2,1)}, u32[]{:S(2)}) copy-start(bf16[8192,16]{0,1:T(8,128)(2,1)} %param.18) | copy-start | bytes 786436
  4.9 6.3 %copy-start.4 = (bf16[8192,16]{0,1:T(8,128)(2,1)S(1)}, bf16[8192,16]{0,1:T(8,128)(2,1)}, u32[]{:S(2)}) copy-start(bf16[8192,16]{0,1:T(8,128)(2,1)} %param.17) | copy-start | bytes 786436
  6.9 92.8 %collective-permute-start = (bf16[1,128]{1,0:T(2,128)(2,1)S(1)}, bf16[1,128]{1,0:T(2,128)(2,1)S(1)}, u32[]{:S(2)}, u32[]{:S(2)}) collective-permute-start(bf16[1,128]{1,0:T(2,128)(2,1)S(1)} %bitcast.334), channel_id=1, source_target_pairs={{0,4},{4,0},{8,12},{12,8},{16,20},{20,16},{24,28},{28,24},{32,36},... | collective-permute-start | bytes 776 | tf_op jit(solution)/shard_map/ppermute | solution.py:15
  10.7 90.1 %collective-permute-start.6 = (bf16[1,128]{1,0:T(2,128)(2,1)S(1)}, bf16[1,128]{1,0:T(2,128)(2,1)S(1)}, u32[]{:S(2)}, u32[]{:S(2)}) collective-permute-start(bf16[1,128]{1,0:T(2,128)(2,1)S(1)} %bitcast.332), channel_id=1, source_target_pairs={{0,4},{4,0},{8,12},{12,8},{16,20},{20,16},{24,28},{28,24},{32,36},... | collective-permute-start | bytes 776 | tf_op jit(solution)/shard_map/ppermute | solution.py:15
  91.8 4.8 %copy-start.2 = (bf16[1,2048,8,128]{3,2,1,0:T(8,128)(2,1)S(1)}, bf16[1,2048,8,128]{3,2,1,0:T(8,128)(2,1)}, u32[]{:S(2)}) copy-start(bf16[1,2048,8,128]{3,2,1,0:T(8,128)(2,1)} %param.21) | copy-start | bytes 12582916
  99.7 2.5 %collective-permute-start.1 = (bf16[1,256]{1,0:T(2,128)(2,1)S(1)}, bf16[1,256]{1,0:T(2,128)(2,1)S(1)}, u32[]{:S(2)}, u32[]{:S(2)}) collective-permute-start(bf16[1,256]{1,0:T(2,128)(2,1)S(1)} %broadcast_select_fusion.9), channel_id=1, source_target_pairs={{0,8},{4,12},{8,0},{12,4},{16,24},{20,28},{24,16},{28,20},{32,40},... | collective-permute-start | bytes 1544 | tf_op jit(solution)/shard_map/ppermute | solution.py:15
  100.7 3.3 %collective-permute-start.7 = (bf16[1,256]{1,0:T(2,128)(2,1)S(1)}, bf16[1,256]{1,0:T(2,128)(2,1)S(1)}, u32[]{:S(2)}, u32[]{:S(2)}) collective-permute-start(bf16[1,256]{1,0:T(2,128)(2,1)S(1)} %broadcast_select_fusion.8), channel_id=1, source_target_pairs={{0,8},{4,12},{8,0},{12,4},{16,24},{20,28},{24,16},{28,20},{32,40},... | collective-permute-start | bytes 1544 | tf_op jit(solution)/shard_map/ppermute | solution.py:15
  102.2 4.0 %collective-permute-start.2 = (bf16[1,512]{1,0:T(2,128)(2,1)S(1)}, bf16[1,512]{1,0:T(2,128)(2,1)S(1)}, u32[]{:S(2)}, u32[]{:S(2)}) collective-permute-start(bf16[1,512]{1,0:T(2,128)(2,1)S(1)} %broadcast_select_fusion.7), channel_id=1, source_target_pairs={{0,16},{4,20},{8,24},{12,28},{16,0},{20,4},{24,8},{28,12},{32,48},... | collective-permute-start | bytes 3080 | tf_op jit(solution)/shard_map/ppermute | solution.py:15
  104.0 4.3 %collective-permute-start.8 = (bf16[1,512]{1,0:T(2,128)(2,1)S(1)}, bf16[1,512]{1,0:T(2,128)(2,1)S(1)}, u32[]{:S(2)}, u32[]{:S(2)}) collective-permute-start(bf16[1,512]{1,0:T(2,128)(2,1)S(1)} %broadcast_select_fusion.6), channel_id=1, source_target_pairs={{0,16},{4,20},{8,24},{12,28},{16,0},{20,4},{24,8},{28,12},{32,48},... | collective-permute-start | bytes 3080 | tf_op jit(solution)/shard_map/ppermute | solution.py:15
  106.3 2.5 %collective-permute-start.3 = (bf16[1,1024]{1,0:T(2,128)(2,1)S(1)}, bf16[1,1024]{1,0:T(2,128)(2,1)S(1)}, u32[]{:S(2)}, u32[]{:S(2)}) collective-permute-start(bf16[1,1024]{1,0:T(2,128)(2,1)S(1)} %broadcast_select_fusion.5), channel_id=1, source_target_pairs={{0,32},{4,36},{8,40},{12,44},{16,48},{20,52},{24,56},{28,60},{32,0... | collective-permute-start | bytes 6152 | tf_op jit(solution)/shard_map/ppermute | solution.py:15
  108.4 2.5 %collective-permute-start.9 = (bf16[1,1024]{1,0:T(2,128)(2,1)S(1)}, bf16[1,1024]{1,0:T(2,128)(2,1)S(1)}, u32[]{:S(2)}, u32[]{:S(2)}) collective-permute-start(bf16[1,1024]{1,0:T(2,128)(2,1)S(1)} %broadcast_select_fusion.4), channel_id=1, source_target_pairs={{0,32},{4,36},{8,40},{12,44},{16,48},{20,52},{24,56},{28,60},{32,0... | collective-permute-start | bytes 6152 | tf_op jit(solution)/shard_map/ppermute | solution.py:15
  108.9 3.7 %collective-permute-start.4 = (bf16[1,2048]{1,0:T(2,128)(2,1)S(1)}, bf16[1,2048]{1,0:T(2,128)(2,1)S(1)}, u32[]{:S(2)}, u32[]{:S(2)}) collective-permute-start(bf16[1,2048]{1,0:T(2,128)(2,1)S(1)} %broadcast_select_fusion.3), channel_id=1, source_target_pairs={{0,64},{4,68},{8,72},{12,76},{16,80},{20,84},{24,88},{28,92},{32,9... | collective-permute-start | bytes 12296 | tf_op jit(solution)/shard_map/ppermute | solution.py:15
  110.9 4.8 %collective-permute-start.10 = (bf16[1,2048]{1,0:T(2,128)(2,1)S(1)}, bf16[1,2048]{1,0:T(2,128)(2,1)S(1)}, u32[]{:S(2)}, u32[]{:S(2)}) collective-permute-start(bf16[1,2048]{1,0:T(2,128)(2,1)S(1)} %broadcast_select_fusion.2), channel_id=1, source_target_pairs={{0,64},{4,68},{8,72},{12,76},{16,80},{20,84},{24,88},{28,92},{32,9... | collective-permute-start | bytes 12296 | tf_op jit(solution)/shard_map/ppermute | solution.py:15
  112.7 6.6 %collective-permute-start.5 = (bf16[1,4096]{1,0:T(2,128)(2,1)S(1)}, bf16[1,4096]{1,0:T(2,128)(2,1)S(1)}, u32[]{:S(2)}, u32[]{:S(2)}) collective-permute-start(bf16[1,4096]{1,0:T(2,128)(2,1)S(1)} %broadcast_select_fusion.1), channel_id=1, source_target_pairs={{0,128},{4,132},{8,136},{12,140},{16,144},{20,148},{24,152},{28,15... | collective-permute-start | bytes 24584 | tf_op jit(solution)/shard_map/ppermute | solution.py:15
  115.8 30.5 %collective-permute-start.11 = (bf16[1,4096]{1,0:T(2,128)(2,1)S(1)}, bf16[1,4096]{1,0:T(2,128)(2,1)S(1)}, u32[]{:S(2)}, u32[]{:S(2)}) collective-permute-start(bf16[1,4096]{1,0:T(2,128)(2,1)S(1)} %broadcast_select_fusion), channel_id=1, source_target_pairs={{0,128},{4,132},{8,136},{12,140},{16,144},{20,148},{24,152},{28,15... | collective-permute-start | bytes 24584 | tf_op jit(solution)/shard_map/ppermute | solution.py:15
  134.4 29.2 %all-to-all-start = ((bf16[1,64,130]{2,0,1:T(2,128)(2,1)}), bf16[1,64,130]{2,0,1:T(2,128)(2,1)S(1)}, u32[]{:S(2)}, u32[]{:S(2)}) async-start(bf16[1,64,130]{2,0,1:T(2,128)(2,1)} %copy.59), calls=%async_computation | async-start | bytes 131072 | tf_op jit(solution)/shard_map/all_to_all | solution.py:35
  163.6 20.4 %all-to-all-start.2 = ((bf16[1,64,130]{2,0,1:T(2,128)(2,1)}), bf16[1,64,130]{2,0,1:T(2,128)(2,1)S(1)}, u32[]{:S(2)}, u32[]{:S(2)}) async-start(bf16[1,64,130]{2,0,1:T(2,128)(2,1)} %copy.65), calls=%async_computation.2 | async-start | bytes 131072 | tf_op jit(solution)/shard_map/all_to_all | solution.py:35
  184.0 13.9 %all-to-all-start.1 = ((f32[64,128,1]{1,2,0:T(1,128)}), f32[64,128,1]{1,2,0:T(1,128)S(1)}, u32[]{:S(2)}, u32[]{:S(2)}) async-start(f32[64,128,1]{1,2,0:T(1,128)} %fusion.42), calls=%async_computation.1 | async-start | bytes 65536 | tf_op jit(solution)/shard_map/all_to_all | solution.py:48
  197.9 16.4 %all-to-all-start.3 = ((f32[64,128,1]{1,2,0:T(1,128)}), f32[64,128,1]{1,2,0:T(1,128)S(1)}, u32[]{:S(2)}, u32[]{:S(2)}) async-start(f32[64,128,1]{1,2,0:T(1,128)} %fusion.45), calls=%async_computation.3 | async-start | bytes 65536 | tf_op jit(solution)/shard_map/all_to_all | solution.py:48
